TPU v7x, 512 devices: a whole 4x4x16 slice. The times are simulated.
512 devices in a mesh: cons: 16 (over y, x), row: 32 (over z, core).
Axes of the slice: x: 4, y: 4, z: 16, core: 2. Of those that a mesh axis runs over, the one named last changes fastest.
Arguments:
- start_primal: float32 [256, 512, 128], P('row', 'cons'), may hold values from 0 to 1
- start_dual: float32 [1024, 128, 128], P(('cons', 'row')), may hold values from 0 to 1
- unit_cost: float32 [256, 512, 128], P('row', 'cons'), may hold values from -6 to 6
- upper_bound: float32 [256, 512, 128], P('row', 'cons'), may hold values from 0.5 to 2
- demand: float32 [1024, 128, 128], P(('cons', 'row')), may hold values from -6 to 6
- tile_values: bfloat16 [8192, 128, 128], P(('cons', 'row')), may hold values from -0.1875 to 0.1875
- tile_rows: int32 [8192], P(('cons', 'row')), may hold values from 0 to 1
- tile_cols: int32 [8192], P(('cons', 'row')), may hold values from 0 to 31
- tile_count: int32 [512], P(('cons', 'row')), may hold values from 8 to 16, as said below
Outputs:
- primal: float32 [256, 512, 128], P('row', 'cons')
- dual: float32 [1024, 128, 128], P(('cons', 'row'))
Inputs may be any that keep to these rules, and one draw needn't show every extreme that they name: `tile_count`: A device's live tiles are the first slots of its list; some device has all 16 slots live.
All inputs are finite; a program needn't handle non-finite values.
Results may differ from a plain program's by a relative error of at most 0.00095.
The roundings to bfloat16 on the way count: a program that leaves them out, or rounds other values in their place, can miss the bound.
Values may be sent and summed in bfloat16 or wider, within the bound.
A program may use at most 128 MiB of HBM per device.

v0:
```python
import jax
import jax.numpy as jnp
from jax import lax
from jax.sharding import PartitionSpec as P

ITERS = 2


step_scale = 0.9


def body(
    start_primal,
    start_dual,
    unit_cost,
    upper_bound,
    demand,
    tile_values,
    tile_rows,
    tile_cols,
    tile_count,
):
    st_local, sku_local, scenes = start_primal.shape
    n_row = lax.axis_size("row")
    n_cons = lax.axis_size("cons")
    sku_dev = sku_local // n_row
    stores = st_local * n_row
    tile_size = tile_values.shape[1]
    slots = tile_values.shape[0]
    blocks_row = start_dual.shape[0]
    panel_blocks = n_cons * sku_dev * stores // tile_size
    live = (jnp.arange(slots) < tile_count[0]).astype(jnp.float32)
    row_hot = (tile_rows[None, :] == jnp.arange(blocks_row)[:, None]).astype(jnp.float32) * live[
        None, :
    ]
    col_hot = (tile_cols[None, :] == jnp.arange(panel_blocks)[:, None]).astype(jnp.float32) * live[
        None, :
    ]

    def make_panel(extrapolated):
        parted = extrapolated.reshape(st_local, n_row, sku_dev, scenes)
        moved = lax.all_to_all(parted, "row", split_axis=1, concat_axis=0, tiled=True)
        moved = moved.reshape(stores, sku_dev, scenes).transpose(1, 0, 2)
        panel = lax.all_gather(moved, "cons", axis=0, tiled=True)
        return panel.reshape(panel_blocks, tile_size, scenes)

    def forward_product(extrapolated):
        panel = make_panel(extrapolated)
        blocks = panel[tile_cols]
        product = lax.dot_general(
            tile_values, blocks, (((2,), (1,)), ((0,), (0,))), preferred_element_type=jnp.float32
        )
        summed = jnp.dot(
            row_hot, product.reshape(slots, tile_size * scenes), precision=lax.Precision.HIGHEST
        )
        return summed.reshape(blocks_row, tile_size, scenes)

    def adjoint_product(dual_low):
        blocks = dual_low[tile_rows]
        product = lax.dot_general(
            tile_values, blocks, (((1,), (1,)), ((0,), (0,))), preferred_element_type=jnp.float32
        )
        partial_value = jnp.dot(
            col_hot, product.reshape(slots, tile_size * scenes), precision=lax.Precision.HIGHEST
        )
        partial_value = partial_value.reshape(n_cons * sku_dev, stores, scenes)
        owned = lax.psum_scatter(partial_value, "cons", scatter_dimension=0, tiled=True)
        owned = owned.reshape(1, sku_dev, n_row, st_local, scenes)
        moved = lax.all_to_all(owned, "row", split_axis=2, concat_axis=0, tiled=True)
        moved = moved.reshape(n_row * sku_dev, st_local, scenes)
        return moved.transpose(1, 0, 2)

    primal = start_primal
    dual = start_dual
    weight_ratio = jnp.float32(1.0)
    for iteration in range(ITERS):
        adjoint = adjoint_product(dual.astype(jnp.bfloat16))
        new_primal = jnp.minimum(
            jnp.maximum(primal - step_scale / weight_ratio * (unit_cost - adjoint), 0.0),
            upper_bound,
        )
        local_primal = jnp.sum((new_primal - primal) ** 2)
        primal_change = local_primal
        if iteration < ITERS - 1:
            primal_change = lax.psum(local_primal, ("cons", "row"))
        extrapolated = (2.0 * new_primal - primal).astype(jnp.bfloat16)
        forward = forward_product(extrapolated)
        new_dual = jnp.maximum(dual + step_scale * weight_ratio * (demand - forward), 0.0)
        if iteration < ITERS - 1:
            local_dual = jnp.sum((new_dual - dual) ** 2)
            dual_change = lax.psum(local_dual, ("cons", "row"))
            weight_ratio = jnp.sqrt(
                weight_ratio * jnp.sqrt((dual_change + 1e-06) / (primal_change + 1e-06))
            )
        primal = new_primal
        dual = new_dual
    return (primal, dual)


def solution(mesh):
    placed = (
        P("row", "cons", None),
        P(("cons", "row"), None, None),
        P("row", "cons", None),
        P("row", "cons", None),
        P(("cons", "row"), None, None),
        P(("cons", "row"), None, None),
        P(("cons", "row")),
        P(("cons", "row")),
        P(("cons", "row")),
    )
    return jax.shard_map(
        body,
        mesh=mesh,
        in_specs=placed,
        out_specs=(P("row", "cons", None), P(("cons", "row"), None, None)),
        check_vma=False,
    )
```

profile of v0, /device:TPU:6, one launch (start us, length us, event | category | flops | bytes accessed | tf_op | source)
XLA Modules:
  0.0 507.8 jit_solution(11607964460980251176)
XLA Ops:
  7.2 0.0 copy-start
  7.2 0.0 reduce-scatter.7.cloned.1.call-start
  7.9 0.7 compare_select_fusion.1
  8.6 0.9 convert_element_type.22
  9.5 0.6 gather_fusion
  10.2 0.0 copy-start.6
  10.2 0.4 convolution_bitcast_fusion.3
  10.6 1.3 copy.71
  11.9 3.4 fusion.3
  15.2 1.5 reshape.68
  16.7 0.0 reduce-scatter.7.cloned.1.call-update
  16.8 0.0 all-gather.3.cloned.1.call-start
  16.8 94.6 %reduce-scatter.7.cloned.1.call-done = f32[1,256,128]{2,1,0:T(8,128)} async-done(((f32[16,256,128]{2,1,0:T(8,128)}), f32[1,256,128]{2,1,0:T(8,128)}) %reduce-scatter.7.cloned.1.call-update) | async-done | bytes 131088
  111.5 29.8 %all_to_all.48 = f32[1,1,32,8,128]{4,3,1,0,2:T(8,128)S(1)} all-to-all(f32[1,1,32,8,128]{4,3,1,0,2:T(8,128)} %bitcast.118), channel_id=1, replica_groups=mesh['cons'=16,'row'=32] {'row'}, dimensions={2} | all-to-all | bytes 262144 | tf_op jit(solution)/shard_map/all_to_all | solution.py:69
  141.2 0.8 multiply_reduce_fusion
  142.1 0.1 fusion.26
  142.2 18.0 %all_to_all.49 = bf16[8,32,1,128]{3,0,2,1:T(8,128)(2,1)} all-to-all(bf16[8,32,1,128]{3,0,2,1:T(8,128)(2,1)S(1)} %fusion.26), channel_id=1, replica_groups=mesh['cons'=16,'row'=32] {'row'}, dimensions={1} | all-to-all | bytes 131072 | tf_op jit(solution)/shard_map/all_to_all | solution.py:42
  160.2 0.0 all-gather.3.cloned.1.call-update
  160.2 0.0 reduce-scatter.9.cloned.1.call-start
  160.2 47.0 %all-gather.3.cloned.1.call-done = bf16[16,256,128]{2,1,0:T(8,128)(2,1)} async-done(((bf16[1,256,128]{2,1,0:T(8,128)(2,1)}), bf16[16,256,128]{2,1,0:T(8,128)(2,1)}) %all-gather.3.cloned.1.call-update) | async-done | bytes 1048592 | tf_op jit(solution)/shard_map/all_gather | solution.py:44
  207.2 1.9 gather_fusion.1
  209.1 0.0 copy-start.7
  209.1 0.5 convolution_bitcast_fusion.2
  209.6 0.0 copy-start.5
  209.7 0.3 copy.79
  210.0 1.2 fusion.9
  211.2 0.6 multiply_reduce_fusion.1
  211.8 0.6 gather_fusion.2
  212.5 0.3 convolution_bitcast_fusion.1
  212.9 1.3 copy.84
  214.2 3.4 fusion
  217.5 1.5 reshape.75
  219.0 0.0 reduce-scatter.9.cloned.1.call-update
  219.1 90.3 %reduce-scatter.9.cloned.1.call-done = f32[1,256,128]{2,1,0:T(8,128)} async-done(((f32[16,256,128]{2,1,0:T(8,128)}), f32[1,256,128]{2,1,0:T(8,128)}) %reduce-scatter.9.cloned.1.call-update) | async-done | bytes 131088
  309.3 12.6 %all-to-all-start.2 = ((f32[1,1,32,8,128]{4,3,1,0,2:T(8,128)}), f32[1,1,32,8,128]{4,3,1,0,2:T(8,128)S(1)}, u32[]{:S(2)}, u32[]{:S(2)}) async-start(f32[1,1,32,8,128]{4,3,1,0,2:T(8,128)} %bitcast.117), calls=%async_computation.2 | async-start | bytes 262144 | tf_op jit(solution)/shard_map/all_to_all | solution.py:69
  321.9 0.0 all-gather.5.cloned.1.call-start
  322.0 103.7 %all-reduce.2 = (f32[]{:T(128)}, f32[]{:T(128)}) all-reduce(f32[]{:T(128)} %get-tuple-element.16, f32[]{:T(128)} %get-tuple-element.14), channel_id=1, replica_groups=mesh['cons'=16,'row'=32] {'cons','row'}, use_global_device_ids=true, to_apply=%region_2.0 | all-reduce | flops 2 | bytes 16 | tf_op jit(solution)/shard_map/psum | solution.py:91
  427.1 0.0 all-to-all-done.2
  427.2 0.2 fusion.27
  427.3 23.1 %all_to_all.50 = bf16[8,32,1,128]{3,0,2,1:T(8,128)(2,1)} all-to-all(bf16[8,32,1,128]{3,0,2,1:T(8,128)(2,1)S(1)} %get-tuple-element.12), channel_id=1, replica_groups=mesh['cons'=16,'row'=32] {'row'}, dimensions={1} | all-to-all | bytes 131072 | tf_op jit(solution)/shard_map/all_to_all | solution.py:42
  450.4 0.0 all-gather.5.cloned.1.call-update
  450.5 0.7 copy.93
  451.1 45.5 %all-gather.5.cloned.1.call-done = bf16[16,256,128]{2,1,0:T(8,128)(2,1)} async-done(((bf16[1,256,128]{2,1,0:T(8,128)(2,1)}), bf16[16,256,128]{2,1,0:T(8,128)(2,1)}) %all-gather.5.cloned.1.call-update) | async-done | bytes 1048592 | tf_op jit(solution)/shard_map/all_gather | solution.py:44
  496.6 1.9 gather_fusion.3
  498.5 0.5 convolution_bitcast_fusion
  499.0 0.3 copy.90
  499.3 1.2 fusion.6
  500.5 0.7 fusion.22
  (16 shorter events, 0.0 us)
Async XLA Ops:
  7.2 3.0 copy-start
  7.2 104.3 %reduce-scatter.7.cloned.1.call-start = ((), (), s32[]{:S(2)}) async-start(), calls=%async_computation.8 | async-start | bytes 2228224
  10.2 1.7 copy-start.6
  16.7 124.5 %copy-start.2 = (f32[8,32,128]{2,1,0:T(8,128)S(1)}, f32[8,32,128]{2,1,0:T(8,128)}, u32[]{:S(2)}) copy-start(f32[8,32,128]{2,1,0:T(8,128)} %param.12) | copy-start | bytes 393220
  16.7 124.5 %copy-start.3 = (f32[8,32,128]{2,1,0:T(8,128)S(1)}, f32[8,32,128]{2,1,0:T(8,128)}, u32[]{:S(2)}) copy-start(f32[8,32,128]{2,1,0:T(8,128)} %param.11) | copy-start | bytes 393220
  16.7 124.5 %copy-start.4 = (f32[8,32,128]{2,1,0:T(8,128)S(1)}, f32[8,32,128]{2,1,0:T(8,128)}, u32[]{:S(2)}) copy-start(f32[8,32,128]{2,1,0:T(8,128)} %param.9) | copy-start | bytes 393220
  16.8 190.5 %all-gather.3.cloned.1.call-start = ((), (), s32[]{:S(2)}) async-start(), calls=%async_computation.6 | async-start | bytes 1114112 | tf_op jit(solution)/shard_map/all_gather | solution.py:44
  160.2 149.2 %reduce-scatter.9.cloned.1.call-start = ((), (), s32[]{:S(2)}) async-start(), calls=%async_computation.9 | async-start | bytes 2228224
  209.1 0.9 copy-start.7
  209.6 1.6 copy-start.1
  209.6 1.6 copy-start.5
  309.3 117.8 %all-to-all-start.2 = ((f32[1,1,32,8,128]{4,3,1,0,2:T(8,128)}), f32[1,1,32,8,128]{4,3,1,0,2:T(8,128)S(1)}, u32[]{:S(2)}, u32[]{:S(2)}) async-start(f32[1,1,32,8,128]{4,3,1,0,2:T(8,128)} %bitcast.117), calls=%async_computation.2 | async-start | bytes 262144 | tf_op jit(solution)/shard_map/all_to_all | solution.py:69
  321.9 174.7 %all-gather.5.cloned.1.call-start = ((), (), s32[]{:S(2)}) async-start(), calls=%async_computation.7 | async-start | bytes 1114112 | tf_op jit(solution)/shard_map/all_gather | solution.py:44
Sparse Core Ops, SparseCore 0:
  16.9 94.5 reduce-scatter.6
  160.3 46.8 all-gather.2
  219.2 90.1 reduce-scatter.8
  450.6 45.9 all-gather.4
where the time goes:
time: 508 us
  waiting for transfers between devices  277 us (55%)
  blocking collectives  175 us (34%)
  between operations  16.1 us (3%)
  starting transfers between devices  12.7 us (2%)
  local copies, waits for them, and re-layouts  12 us (2%)
  matrix products  10.8 us (2%)
    unnamed x6, waiting for transfers between devices  185 us
    psum x1, blocking collectives, body(): dual_change = lax.psum(local_dual, ('cons', 'row'))  104 us
    all_gather x2, waiting for transfers between devices, make_panel(): panel = lax.all_gather(moved, 'cons', axis=0, tiled=True)  92.4 us
    all_to_all x2, blocking collectives, make_panel(): lax.all_to_all(parted, 'row', split_axis=1, concat_axis=0, tiled=True)  41.1 us
    all_to_all x1, blocking collectives, adjoint_product(): lax.all_to_all(owned, 'row', split_axis=2, concat_axis=0, tiled=True)  29.8 us
    all_to_all x1, starting transfers between devices, adjoint_product(): lax.all_to_all(owned, 'row', split_axis=2, concat_axis=0, tiled=True)  12.6 us
  transfers between devices with their start and end apart: 5, of which 4 were waited for; matrix products, arithmetic and copies ran while one was open for 0% of the time, Pallas kernels for 0%

commit v1 on v0

v1 whole, which is shorter than its diff:
```python
import functools

import jax
import jax.numpy as jnp
from jax import lax
from jax.experimental import pallas as pl
from jax.experimental.pallas import tpu as pltpu
from jax.sharding import PartitionSpec as P

ITERS = 2
step_scale = 0.9
SIDE = 4
MESH = pl.DeviceIdType.MESH
F32 = jnp.float32
BF16 = jnp.bfloat16
MSGS = 80


def kernel(
    n_row,
    slots,
    meta,
    hot,
    primal_in,
    cost_in,
    bound_in,
    dual_in,
    demand_in,
    tiles,
    primal_out,
    dual_out,
    zs,
    zr,
    chain,
    part,
    r1,
    l1,
    r2,
    l2,
    mid,
    q1r,
    q1l,
    q2r,
    q2l,
    panel,
    newp,
    outb,
    dlow,
    ar_s,
    ar1,
    ar2,
    ar3,
    send_sem,
    recv_sem,
    z_send,
    z_recv,
):
    st_local = primal_in.shape[0] // n_row
    tile = tiles.shape[1]
    half = tile // 2
    me_c = lax.axis_index("cons")
    me_r = lax.axis_index("row")
    y = me_c // SIDE
    x = me_c % SIDE

    def at_xy(yy, xx):
        return lax.rem(yy, SIDE) * SIDE + lax.rem(xx, SIDE)

    x_next, x_prev = at_xy(y, x + 1), at_xy(y, x + 3)
    y_next, y_prev = at_xy(y + 1, x), at_xy(y + 3, x)
    pos_a, pos_b = (x, y), (y, x)
    next_a, prev_a = (x_next, y_next), (x_prev, y_prev)
    next_b, prev_b = (y_next, x_next), (y_prev, x_prev)

    def blk(color, b, a):
        return at_xy(b, a) if color == 0 else at_xy(a, b)

    barrier = pltpu.get_barrier_semaphore()

    def greet(i, carry):
        pl.semaphore_signal(
            barrier, inc=1, device_id=(me_c, lax.rem(me_r + i, n_row)), device_id_type=MESH
        )
        return carry

    for i in range(1, SIDE):
        pl.semaphore_signal(barrier, inc=1, device_id=(at_xy(y, x + i), me_r), device_id_type=MESH)
        pl.semaphore_signal(barrier, inc=1, device_id=(at_xy(y + i, x), me_r), device_id_type=MESH)
    lax.fori_loop(1, n_row, greet, 0)

    pending = []
    counter = [0]

    def send(src, dst, target):
        i = counter[0]
        counter[0] += 1
        copy = pltpu.make_async_remote_copy(
            src_ref=src,
            dst_ref=dst,
            send_sem=send_sem.at[i],
            recv_sem=recv_sem.at[i],
            device_id=(target, me_r),
            device_id_type=MESH,
        )
        copy.start()
        pending.append(copy)
        return copy

    for j in range(n_row):
        for k, ref in enumerate((primal_in, cost_in, bound_in)):
            zs[j, k * st_local : (k + 1) * st_local, :] = ref[pl.ds(j, st_local, stride=n_row), :]

    def adjoint(it):
        for r in range(2):
            src = dual_in if it == 0 else dual_out
            dlow[it, r] = src[r].astype(BF16)
        for t in range(slots):
            row = meta[slots + t]
            prod = lax.dot_general(
                tiles[t], dlow[it, row], (((0,), (0,)), ((), ())), preferred_element_type=F32
            )
            chain[t] = prod + chain[meta[2 * slots + t]]
        for b in range(2 * SIDE * SIDE):
            part[it, b // 2, b % 2] = chain[meta[3 * slots + b]]

    OFF = (2, 1, 3, 0)

    def scatter_sum(it, mids):
        first = {}
        for k in range(4):
            for c in range(2):
                opp = part.at[it, blk(c, pos_b[c] + OFF[k], pos_a[c] + 2), c]
                a = send(opp.at[pl.ds(0, half)], r1.at[it, c, k], next_a[c])
                b = send(opp.at[pl.ds(half, half)], l1.at[it, c, k], prev_a[c])
                first[k, c] = (a, b)
        second = {}
        for k in range(4):
            for c in range(2):
                a, b = first[k, c]
                nb = blk(c, pos_b[c] + OFF[k], pos_a[c] + 1)
                a.wait_recv()
                part[it, nb, c, 0:half, :] = part[it, nb, c, 0:half, :] + r1[it, c, k]
                a2 = send(part.at[it, nb, c], r2.at[it, c, k], next_a[c])
                pb = blk(c, pos_b[c] + OFF[k], pos_a[c] + 3)
                b.wait_recv()
                part[it, pb, c, half:tile, :] = part[it, pb, c, half:tile, :] + l1[it, c, k]
                b2 = send(part.at[it, pb, c], l2.at[it, c, k], prev_a[c])
                second[k, c] = (a2, b2)
        mids(0)
        third, fourth = {}, {}
        for k in range(4):
            for c in range(2):
                a, b = second[k, c]
                a.wait_recv()
                b.wait_recv()
                own = blk(c, pos_b[c] + OFF[k], pos_a[c])
                total = part[it, own, c] + r2[it, c, k] + l2[it, c, k]
                if k == 0:
                    mid[it, c, 0] = total
                    s0 = mid.at[it, c, 0]
                    third[c] = (
                        send(s0.at[pl.ds(0, half)], q1r.at[it, c], next_b[c]),
                        send(s0.at[pl.ds(half, half)], q1l.at[it, c], prev_b[c]),
                    )
                elif k == 1:
                    third[c][0].wait_recv()
                    mid[it, c, 1, half:tile, :] = total[half:tile]
                    mid[it, c, 1, 0:half, :] = total[0:half] + q1r[it, c]
                    fourth[c] = [send(mid.at[it, c, 1], q2r.at[it, c], next_b[c])]
                elif k == 2:
                    third[c][1].wait_recv()
                    mid[it, c, 2, 0:half, :] = total[0:half]
                    mid[it, c, 2, half:tile, :] = total[half:tile] + q1l[it, c]
                    fourth[c].append(send(mid.at[it, c, 2], q2l.at[it, c], prev_b[c]))
                else:
                    mid[it, c, 3] = total
        mids(1)
        return fourth

    def finish_sum(it, c, fourth):
        fourth[c][0].wait_recv()
        fourth[c][1].wait_recv()
        return mid[it, c, 3] + q2r[it, c] + q2l[it, c]

    def gather_start(it, c):
        own = panel.at[it, me_c, c]
        return (
            send(own, own, next_b[c]),
            send(own, own, prev_b[c]),
            send(own, own, next_a[c]),
            send(own, own, prev_a[c]),
        )

    def gather_rest(it, starts):
        lo, hi = pl.ds(0, half), pl.ds(half, half)
        deep = {}
        wide = {c: [(0, starts[c][2], starts[c][3])] for c in range(2)}

        def spread(c, b_off):
            piece = panel.at[it, blk(c, pos_b[c] + b_off, pos_a[c]), c]
            wide[c].append((b_off, send(piece, piece, next_a[c]), send(piece, piece, prev_a[c])))

        for c in range(2):
            starts[c][0].wait_recv()
            piece = panel.at[it, blk(c, pos_b[c] + 3, pos_a[c]), c]
            f = send(piece.at[lo], piece.at[lo], next_b[c])
            starts[c][1].wait_recv()
            piece = panel.at[it, blk(c, pos_b[c] + 1, pos_a[c]), c]
            g = send(piece.at[hi], piece.at[hi], prev_b[c])
            deep[c] = (f, g)
            spread(c, 3)
            spread(c, 1)
        last = []

        def relay(c, entry):
            b_off, f, g = entry
            f.wait_recv()
            piece = panel.at[it, blk(c, pos_b[c] + b_off, pos_a[c] + 3), c]
            last.append(send(piece.at[lo], piece.at[lo], next_a[c]))
            g.wait_recv()
            piece = panel.at[it, blk(c, pos_b[c] + b_off, pos_a[c] + 1), c]
            last.append(send(piece.at[hi], piece.at[hi], prev_a[c]))

        for c in range(2):
            relay(c, wide[c][0])
        for c in range(2):
            deep[c][0].wait_recv()
            deep[c][1].wait_recv()
            spread(c, 2)
        for k in range(1, 4):
            for c in range(2):
                relay(c, wide[c][k])
        for copy in last:
            copy.wait_recv()

    def forward(it, r):
        acc = None
        for t in range(slots):
            prod = jnp.dot(
                tiles[t], panel_at(it, meta[t]), preferred_element_type=F32
            )
            prod = prod * hot[r * slots + t]
            acc = prod if acc is None else acc + prod
        return acc

    def panel_at(it, col):
        return panel[it, col // 2, col % 2]

    chain[slots] = jnp.zeros((tile, tile), F32)
    adjoint(0)
    pl.semaphore_wait(barrier, (n_row - 1) + 2 * (SIDE - 1))

    def row_copy(src, dst, group, i):
        return pltpu.make_async_remote_copy(
            src_ref=src,
            dst_ref=dst,
            send_sem=z_send.at[group],
            recv_sem=z_recv.at[group],
            device_id=(me_c, lax.rem(me_r + i, n_row)),
            device_id_type=MESH,
        )

    def send_in(i, carry):
        row_copy(zs.at[lax.rem(me_r + i, n_row)], zr.at[me_r], 0, i).start()
        return carry

    def wait_rows(buf, group):
        everything = buf.at[pl.ds(0, n_row - 1)]
        pltpu.make_async_copy(everything, everything, z_recv.at[group]).wait()

    def wait_rows_sent(buf, group):
        everything = buf.at[pl.ds(0, n_row - 1)]
        pltpu.make_async_copy(everything, everything, z_send.at[group]).wait()

    lax.fori_loop(1, n_row, send_in, 0)
    zr[me_r] = zs[me_r]
    fourth = scatter_sum(0, lambda stage: None)
    wait_rows(zr, 0)
    starts = {}
    blocks = n_row // 2
    p_change = None
    for c in range(2):
        adj = finish_sum(0, c, fourth)
        rows = pl.ds(c * blocks, blocks)
        old = zr[rows, 0:st_local, :].reshape(tile, tile)
        cost = zr[rows, st_local : 2 * st_local, :].reshape(tile, tile)
        bound = zr[rows, 2 * st_local : 3 * st_local, :].reshape(tile, tile)
        new = jnp.minimum(jnp.maximum(old - step_scale * (cost - adj), 0.0), bound)
        newp[0, c] = new
        panel[0, me_c, c] = (2.0 * new - old).astype(BF16)
        starts[c] = gather_start(0, c)
        moved = jnp.sum((new - old) ** 2, axis=0, keepdims=True)
        p_change = moved if p_change is None else p_change + moved
    gather_rest(0, starts)
    d_change = None
    for r in range(2):
        old = dual_in[r]
        new = jnp.maximum(old + step_scale * (demand_in[r] - forward(0, r)), 0.0)
        dual_out[r] = new
        moved = jnp.sum((new - old) ** 2, axis=0, keepdims=True)
        d_change = moved if d_change is None else d_change + moved
    line = lax.broadcasted_iota(jnp.int32, (8, tile), 0)
    ar_s[0] = jnp.where(
        line == 0,
        jnp.broadcast_to(p_change, (8, tile)),
        jnp.where(line == 1, jnp.broadcast_to(d_change, (8, tile)), 0.0),
    )

    def send_change(i, carry):
        row_copy(ar_s.at[0], ar1.at[me_r], 1, i).start()
        return carry

    lax.fori_loop(1, n_row, send_change, 0)
    ar1[me_r] = ar_s[0]

    adjoint(1)
    counter[0] = MSGS
    sides = {}

    def mids(stage):
        if stage == 0:
            wait_rows(ar1, 1)
            total = ar1[0]
            for i in range(1, n_row):
                total = total + ar1[i]
            ar_s[1] = total
            ar2[x] = total
            sides[0] = [send(ar_s.at[1], ar2.at[x], at_xy(y, x + i)) for i in range(1, SIDE)]
        else:
            for copy in sides[0]:
                copy.wait_recv()
            total = (ar2[0] + ar2[1]) + (ar2[2] + ar2[3])
            ar_s[2] = total
            ar3[y] = total
            sides[1] = [send(ar_s.at[2], ar3.at[y], at_xy(y + i, x)) for i in range(1, SIDE)]

    fourth = scatter_sum(1, mids)
    for copy in sides[1]:
        copy.wait_recv()
    total = (ar3[0] + ar3[1]) + (ar3[2] + ar3[3])
    p_total = jnp.sum(total[0:1], axis=1, keepdims=True)
    d_total = jnp.sum(total[1:2], axis=1, keepdims=True)
    ratio = jnp.sqrt(jnp.sqrt((d_total + 1e-06) / (p_total + 1e-06)))
    p_step = step_scale / ratio
    d_step = step_scale * ratio
    for c in range(2):
        adj = finish_sum(1, c, fourth)
        rows = pl.ds(c * blocks, blocks)
        old = newp[0, c]
        cost = zr[rows, st_local : 2 * st_local, :].reshape(tile, tile)
        bound = zr[rows, 2 * st_local : 3 * st_local, :].reshape(tile, tile)
        new = jnp.minimum(jnp.maximum(old - p_step * (cost - adj), 0.0), bound)
        newp[1, c] = new
        panel[1, me_c, c] = (2.0 * new - old).astype(BF16)
        starts[c] = gather_start(1, c)

    def result_block(j):
        return newp.at[1, j // blocks, pl.ds((j % blocks) * st_local, st_local)]

    def send_out(i, carry):
        row_copy(
            result_block(lax.rem(me_r + i, n_row)),
            outb.at[pl.ds(pl.multiple_of(me_r * st_local, st_local), st_local)],
            2,
            i,
        ).start()
        return carry

    lax.fori_loop(1, n_row, send_out, 0)
    outb[pl.ds(pl.multiple_of(me_r * st_local, st_local), st_local), :] = newp[
        1, me_r // blocks, pl.ds(pl.multiple_of((me_r % blocks) * st_local, st_local), st_local), :
    ]
    gather_rest(1, starts)
    for r in range(2):
        dual_out[r] = jnp.maximum(
            dual_out[r] + d_step * (demand_in[r] - forward(1, r)), 0.0
        )
    everything = outb.at[pl.ds(0, (n_row - 1) * st_local)]
    pltpu.make_async_copy(everything, everything, z_recv.at[2]).wait()
    for s in range(st_local):
        primal_out[s * n_row : (s + 1) * n_row, :] = outb[pl.ds(s, n_row, stride=st_local), :]
    for copy in pending:
        copy.wait_send()
    wait_rows_sent(zs, 0)
    wait_rows_sent(ar1, 1)
    pltpu.make_async_copy(everything, everything, z_send.at[2]).wait()


def body(
    start_primal,
    start_dual,
    unit_cost,
    upper_bound,
    demand,
    tile_values,
    tile_rows,
    tile_cols,
    tile_count,
):
    st_local, sku_local, scenes = start_primal.shape
    n_row = lax.axis_size("row")
    n_cons = lax.axis_size("cons")
    stores = st_local * n_row
    tile = tile_values.shape[1]
    slots = tile_values.shape[0]
    panel_blocks = n_cons * stores // tile
    order = jnp.arange(slots)
    live = order < tile_count[0]
    row_hot = (tile_rows[None, :] == jnp.arange(2)[:, None]) & live[None, :]
    same = (tile_cols[None, :] == tile_cols[:, None]) & (order[None, :] < order[:, None])
    before = jnp.max(jnp.where(same, order[None, :], -1), axis=1)
    before = jnp.where(before < 0, slots, before)
    holds = (tile_cols[None, :] == jnp.arange(panel_blocks)[:, None]) & live[None, :]
    last = jnp.max(jnp.where(holds, order[None, :], -1), axis=1)
    last = jnp.where(last < 0, slots, last)
    meta = jnp.concatenate([tile_cols, tile_rows, before, last]).astype(jnp.int32)
    hot = row_hot.astype(F32).reshape(-1)

    flat = (st_local * sku_local, scenes)
    smem = pl.BlockSpec(memory_space=pltpu.SMEM)
    vmem = pl.BlockSpec(memory_space=pltpu.VMEM)
    total = 2 * MSGS + 2 * (SIDE - 1)
    primal, dual = pl.pallas_call(
        functools.partial(kernel, n_row, slots),
        out_shape=(
            jax.ShapeDtypeStruct(flat, F32),
            jax.ShapeDtypeStruct(start_dual.shape, F32),
        ),
        in_specs=[smem, smem] + [vmem] * 6,
        out_specs=(vmem, vmem),
        scratch_shapes=[
            pltpu.VMEM((n_row, 3 * st_local, scenes), F32),
            pltpu.VMEM((n_row, 3 * st_local, scenes), F32),
            pltpu.VMEM((slots + 1, tile, scenes), F32),
            pltpu.VMEM((2, n_cons, 2, tile, scenes), F32),
            pltpu.VMEM((2, 2, 4, tile // 2, scenes), F32),
            pltpu.VMEM((2, 2, 4, tile // 2, scenes), F32),
            pltpu.VMEM((2, 2, 4, tile, scenes), F32),
            pltpu.VMEM((2, 2, 4, tile, scenes), F32),
            pltpu.VMEM((2, 2, 4, tile, scenes), F32),
            pltpu.VMEM((2, 2, tile // 2, scenes), F32),
            pltpu.VMEM((2, 2, tile // 2, scenes), F32),
            pltpu.VMEM((2, 2, tile, scenes), F32),
            pltpu.VMEM((2, 2, tile, scenes), F32),
            pltpu.VMEM((2, n_cons, 2, tile, scenes), BF16),
            pltpu.VMEM((2, 2, tile, scenes), F32),
            pltpu.VMEM((stores, scenes), F32),
            pltpu.VMEM((2, 2, tile, scenes), BF16),
            pltpu.VMEM((3, 8, scenes), F32),
            pltpu.VMEM((n_row, 8, scenes), F32),
            pltpu.VMEM((SIDE, 8, scenes), F32),
            pltpu.VMEM((SIDE, 8, scenes), F32),
            pltpu.SemaphoreType.DMA((total,)),
            pltpu.SemaphoreType.DMA((total,)),
            pltpu.SemaphoreType.DMA((3,)),
            pltpu.SemaphoreType.DMA((3,)),
        ],
        compiler_params=pltpu.CompilerParams(
            collective_id=0, has_side_effects=True, vmem_limit_bytes=48 * 1024 * 1024
        ),
    )(
        meta,
        hot,
        start_primal.reshape(flat),
        unit_cost.reshape(flat),
        upper_bound.reshape(flat),
        start_dual,
        demand,
        tile_values,
    )
    return (primal.reshape(start_primal.shape), dual)


def solution(mesh):
    placed = (
        P("row", "cons", None),
        P(("cons", "row"), None, None),
        P("row", "cons", None),
        P("row", "cons", None),
        P(("cons", "row"), None, None),
        P(("cons", "row"), None, None),
        P(("cons", "row")),
        P(("cons", "row")),
        P(("cons", "row")),
    )
    return jax.shard_map(
        body,
        mesh=mesh,
        in_specs=placed,
        out_specs=(P("row", "cons", None), P(("cons", "row"), None, None)),
        check_vma=False,
    )
```

time: 508 us -> 97.7 us (0.19)
  waiting for transfers between devices: 277 us -> 0 us
  blocking collectives: 175 us -> 0 us
  Pallas kernels: 0 us -> 86.7 us
  between operations: 16.1 us -> 1.32 us
  starting transfers between devices: 12.7 us -> 0 us
  matrix products: 10.8 us -> 0 us
    unnamed x6 -> x0, waiting for transfers between devices: 185 us -> none
    psum x1 -> x0, blocking collectives: 104 us -> none  [body(): dual_change = lax.psum(local_dual, ('cons', 'row'))]
    all_gather x2 -> x0, waiting for transfers between devices: 92.4 us -> none  [make_panel(): panel = lax.all_gather(moved, 'cons', axis=0, tiled=True)]
    pallas_call x0 -> x1, Pallas kernels: none -> 86.7 us  [body(): pl.pallas_call(functools.partial(kernel, n_row, slots), out_shape=(jax.Sh...]
    all_to_all x3 -> x0, blocking collectives: 70.9 us -> none  [the longest x2 41.1 us: make_panel(): lax.all_to_all(parted, 'row', split_axis=1, concat_axis=0, tiled=True)]
    all_to_all x1 -> x0, starting transfers between devices: 12.6 us -> none  [adjoint_product(): lax.all_to_all(owned, 'row', split_axis=2, concat_axis=0, tiled=True)]
    dot_general x8 -> x0, matrix products: 10.8 us -> none  [the longest x2 6.7 us: adjoint_product(): jnp.dot(col_hot, product.reshape(slots, tile_size * scenes), precision=la...]
    unnamed x17 -> x18, local copies, waits for them, and re-layouts: 0.72 us -> 8.16 us
  transfers between devices with their start and end apart: 5 -> 0, of which waited for: 4 -> 0; matrix products, arithmetic and copies ran while one was open for 0% -> 0% of each run, Pallas kernels for 0% -> 0%
where the time goes in v1:
time: 97.7 us; the launch traced here: 96.6 us
  Pallas kernels  86.7 us (89%)
  local copies, waits for them, and re-layouts  8.25 us (8%)
  between operations  1.32 us (1%)
    pallas_call x1, Pallas kernels, body(): pl.pallas_call(functools.partial(kernel, n_row, slots), out_shape=(jax.Sh...  86.7 us
    unnamed x18, local copies, waits for them, and re-layouts  8.16 us

profile of v1, /device:TPU:6, one launch (start us, length us, event | category | flops | bytes accessed | tf_op | source)
XLA Modules:
  0.0 96.6 jit_solution(16856205323721456818)
XLA Ops:
  1.3 0.0 copy-start.7
  1.3 0.6 copy-done.7
  1.9 0.1 select_reduce_fusion
  2.0 0.0 copy-start.6
  2.1 0.6 copy-done.6
  2.7 0.1 reshape.35.hot
  2.8 0.2 select_reduce_fusion.1
  3.0 0.1 pad_add_fusion.meta
  3.1 0.0 copy-start
  3.1 1.0 %copy-done = bf16[16,128,128]{2,1,0:T(8,128)(2,1)S(1)} copy-done((bf16[16,128,128]{2,1,0:T(8,128)(2,1)S(1)}, bf16[16,128,128]{2,1,0:T(8,128)(2,1)}, u32[]{:S(2)}) %copy-start) | copy-done | bytes 524312
  4.1 0.0 copy-start.1
  4.1 0.9 copy-done.1
  5.0 0.0 copy-start.2
  5.0 0.9 copy-done.2
  5.9 0.0 copy-start.3
  5.9 0.9 copy-done.3
  6.8 0.0 copy-start.4
  6.8 0.9 copy-done.4
  7.7 0.0 copy-start.5
  7.7 0.9 copy-done.5
  8.6 86.7 %shard_map.104 = (f32[256,128]{1,0:T(8,128)S(1)}, f32[2,128,128]{2,1,0:T(8,128)S(1)}) custom-call(s32[80]{0:T(128)S(1)} %pad_add_fusion.meta, f32[32]{0:T(128)S(1)} %reshape.35.hot, f32[256,128]{1,0:T(8,128)S(1)} %bitcast.7, f32[256,128]{1,0:T(8,128)S(1)} %bitcast.8, f32[256,128]{1,0:T(8,128)S(1)} %bitcast.9, f32[2,128,128]{2,1,0:T(8,128)S(1)} %copy-done.4, ...), custom_call_target="tpu_custom_call" | custom-call | tf_op jit(solution)/shard_map/pallas_call | solution.py:423
  95.3 0.7 copy.14
  96.0 0.7 copy.15
  (4 shorter events, 0.0 us)
Async XLA Ops:
  1.3 0.7 copy-start.7
  2.0 0.7 copy-start.6
  3.1 1.0 %copy-start = (bf16[16,128,128]{2,1,0:T(8,128)(2,1)S(1)}, bf16[16,128,128]{2,1,0:T(8,128)(2,1)}, u32[]{:S(2)}) copy-start(bf16[16,128,128]{2,1,0:T(8,128)(2,1)} %tiles.1) | copy-start | bytes 1572868
  4.1 0.9 copy-start.1
  5.0 0.9 copy-start.2
  5.9 0.9 copy-start.3
  6.8 0.9 copy-start.4
  7.7 0.9 copy-start.5

commit v2 on v1

--- a/solution.py
+++ b/solution.py
@@ -13,20 +13,21 @@
 MESH = pl.DeviceIdType.MESH
 F32 = jnp.float32
 BF16 = jnp.bfloat16
-MSGS = 80
+MSGS = 68
 
 
 def kernel(
     n_row,
+    n_cons,
     slots,
     meta,
     hot,
-    primal_in,
-    cost_in,
-    bound_in,
-    dual_in,
-    demand_in,
-    tiles,
+    primal_hbm,
+    cost_hbm,
+    bound_hbm,
+    dual_hbm,
+    demand_hbm,
+    tiles_hbm,
     primal_out,
     dual_out,
     zs,
@@ -38,10 +39,7 @@
     r2,
     l2,
     mid,
-    q1r,
-    q1l,
-    q2r,
-    q2l,
+    near,
     panel,
     newp,
     outb,
@@ -49,12 +47,33 @@
     ar_s,
     ar1,
     ar2,
-    ar3,
     send_sem,
     recv_sem,
     z_send,
     z_recv,
+    primal_in,
+    cost_in,
+    bound_in,
+    dual_in,
+    demand_in,
+    tiles,
+    in_sem,
 ):
+    loads = [
+        pltpu.make_async_copy(src, dst, in_sem.at[i])
+        for i, (src, dst) in enumerate(
+            (
+                (dual_hbm, dual_in),
+                (tiles_hbm, tiles),
+                (primal_hbm, primal_in),
+                (cost_hbm, cost_in),
+                (bound_hbm, bound_in),
+                (demand_hbm, demand_in),
+            )
+        )
+    ]
+    for load in loads:
+        load.start()
     st_local = primal_in.shape[0] // n_row
     tile = tiles.shape[1]
     half = tile // 2
@@ -70,23 +89,30 @@
     y_next, y_prev = at_xy(y + 1, x), at_xy(y + 3, x)
     pos_a, pos_b = (x, y), (y, x)
     next_a, prev_a = (x_next, y_next), (x_prev, y_prev)
-    next_b, prev_b = (y_next, x_next), (y_prev, x_prev)
 
     def blk(color, b, a):
         return at_xy(b, a) if color == 0 else at_xy(a, b)
 
+    def far_first(i):
+        step = i // 2
+        return n_row // 2 + step - 2 * step * (i % 2)
+
     barrier = pltpu.get_barrier_semaphore()
 
     def greet(i, carry):
         pl.semaphore_signal(
-            barrier, inc=1, device_id=(me_c, lax.rem(me_r + i, n_row)), device_id_type=MESH
-        )
-        return carry
-
-    for i in range(1, SIDE):
-        pl.semaphore_signal(barrier, inc=1, device_id=(at_xy(y, x + i), me_r), device_id_type=MESH)
-        pl.semaphore_signal(barrier, inc=1, device_id=(at_xy(y + i, x), me_r), device_id_type=MESH)
+            barrier, inc=1, device_id=(me_c, lax.rem(me_r + far_first(i), n_row)), device_id_type=MESH
+        )
+        return carry
+
+    def greet_cons(i, carry):
+        pl.semaphore_signal(
+            barrier, inc=1, device_id=(lax.rem(me_c + i, n_cons), me_r), device_id_type=MESH
+        )
+        return carry
+
     lax.fori_loop(1, n_row, greet, 0)
+    lax.fori_loop(1, n_cons, greet_cons, 0)
 
     pending = []
     counter = [0]
@@ -106,6 +132,8 @@
         pending.append(copy)
         return copy
 
+    for load in loads[2:5]:
+        load.wait()
     for j in range(n_row):
         for k, ref in enumerate((primal_in, cost_in, bound_in)):
             zs[j, k * st_local : (k + 1) * st_local, :] = ref[pl.ds(j, st_local, stride=n_row), :]
@@ -124,6 +152,8 @@
             part[it, b // 2, b % 2] = chain[meta[3 * slots + b]]
 
     OFF = (2, 1, 3, 0)
+    peers_a = [[at_xy(y, x + o), at_xy(y + o, x)] for o in range(SIDE)]
+    peers_b = [[at_xy(y + o, x), at_xy(y, x + o)] for o in range(SIDE)]
 
     def scatter_sum(it, mids):
         first = {}
@@ -147,90 +177,40 @@
                 b2 = send(part.at[it, pb, c], l2.at[it, c, k], prev_a[c])
                 second[k, c] = (a2, b2)
         mids(0)
-        third, fourth = {}, {}
+        third = {0: [], 1: []}
         for k in range(4):
             for c in range(2):
                 a, b = second[k, c]
                 a.wait_recv()
                 b.wait_recv()
                 own = blk(c, pos_b[c] + OFF[k], pos_a[c])
-                total = part[it, own, c] + r2[it, c, k] + l2[it, c, k]
-                if k == 0:
-                    mid[it, c, 0] = total
-                    s0 = mid.at[it, c, 0]
-                    third[c] = (
-                        send(s0.at[pl.ds(0, half)], q1r.at[it, c], next_b[c]),
-                        send(s0.at[pl.ds(half, half)], q1l.at[it, c], prev_b[c]),
+                mid[it, c, k] = part[it, own, c] + r2[it, c, k] + l2[it, c, k]
+                if k < 3:
+                    third[c].append(
+                        send(mid.at[it, c, k], near.at[it, c, k], peers_b[OFF[k]][c])
                     )
-                elif k == 1:
-                    third[c][0].wait_recv()
-                    mid[it, c, 1, half:tile, :] = total[half:tile]
-                    mid[it, c, 1, 0:half, :] = total[0:half] + q1r[it, c]
-                    fourth[c] = [send(mid.at[it, c, 1], q2r.at[it, c], next_b[c])]
-                elif k == 2:
-                    third[c][1].wait_recv()
-                    mid[it, c, 2, 0:half, :] = total[0:half]
-                    mid[it, c, 2, half:tile, :] = total[half:tile] + q1l[it, c]
-                    fourth[c].append(send(mid.at[it, c, 2], q2l.at[it, c], prev_b[c]))
-                else:
-                    mid[it, c, 3] = total
         mids(1)
-        return fourth
-
-    def finish_sum(it, c, fourth):
-        fourth[c][0].wait_recv()
-        fourth[c][1].wait_recv()
-        return mid[it, c, 3] + q2r[it, c] + q2l[it, c]
+        return third
+
+    def finish_sum(it, c, third):
+        for copy in third[c]:
+            copy.wait_recv()
+        return (mid[it, c, 3] + near[it, c, 0]) + (near[it, c, 1] + near[it, c, 2])
 
     def gather_start(it, c):
         own = panel.at[it, me_c, c]
-        return (
-            send(own, own, next_b[c]),
-            send(own, own, prev_b[c]),
-            send(own, own, next_a[c]),
-            send(own, own, prev_a[c]),
-        )
+        deep = [send(own, own, peers_b[OFF[k]][c]) for k in range(3)]
+        wide = [send(own, own, peers_a[OFF[k]][c]) for k in range(3)]
+        return deep, wide
 
     def gather_rest(it, starts):
-        lo, hi = pl.ds(0, half), pl.ds(half, half)
-        deep = {}
-        wide = {c: [(0, starts[c][2], starts[c][3])] for c in range(2)}
-
-        def spread(c, b_off):
-            piece = panel.at[it, blk(c, pos_b[c] + b_off, pos_a[c]), c]
-            wide[c].append((b_off, send(piece, piece, next_a[c]), send(piece, piece, prev_a[c])))
-
-        for c in range(2):
-            starts[c][0].wait_recv()
-            piece = panel.at[it, blk(c, pos_b[c] + 3, pos_a[c]), c]
-            f = send(piece.at[lo], piece.at[lo], next_b[c])
-            starts[c][1].wait_recv()
-            piece = panel.at[it, blk(c, pos_b[c] + 1, pos_a[c]), c]
-            g = send(piece.at[hi], piece.at[hi], prev_b[c])
-            deep[c] = (f, g)
-            spread(c, 3)
-            spread(c, 1)
-        last = []
-
-        def relay(c, entry):
-            b_off, f, g = entry
-            f.wait_recv()
-            piece = panel.at[it, blk(c, pos_b[c] + b_off, pos_a[c] + 3), c]
-            last.append(send(piece.at[lo], piece.at[lo], next_a[c]))
-            g.wait_recv()
-            piece = panel.at[it, blk(c, pos_b[c] + b_off, pos_a[c] + 1), c]
-            last.append(send(piece.at[hi], piece.at[hi], prev_a[c]))
-
-        for c in range(2):
-            relay(c, wide[c][0])
-        for c in range(2):
-            deep[c][0].wait_recv()
-            deep[c][1].wait_recv()
-            spread(c, 2)
-        for k in range(1, 4):
+        wide = []
+        for k in (1, 2, 0):
             for c in range(2):
-                relay(c, wide[c][k])
-        for copy in last:
+                starts[c][0][k].wait_recv()
+                piece = panel.at[it, blk(c, pos_b[c] + SIDE - OFF[k], pos_a[c]), c]
+                wide += [send(piece, piece, peers_a[OFF[j]][c]) for j in range(3)]
+        for copy in starts[0][1] + starts[1][1] + wide:
             copy.wait_recv()
 
     def forward(it, r):
@@ -247,8 +227,11 @@
         return panel[it, col // 2, col % 2]
 
     chain[slots] = jnp.zeros((tile, tile), F32)
+    loads[0].wait()
+    loads[1].wait()
     adjoint(0)
-    pl.semaphore_wait(barrier, (n_row - 1) + 2 * (SIDE - 1))
+    loads[5].wait()
+    pl.semaphore_wait(barrier, (n_row - 1) + (n_cons - 1))
 
     def row_copy(src, dst, group, i):
         return pltpu.make_async_remote_copy(
@@ -260,7 +243,8 @@
             device_id_type=MESH,
         )
 
-    def send_in(i, carry):
+    def send_in(n, carry):
+        i = far_first(n)
         row_copy(zs.at[lax.rem(me_r + i, n_row)], zr.at[me_r], 0, i).start()
         return carry
 
@@ -274,13 +258,13 @@
 
     lax.fori_loop(1, n_row, send_in, 0)
     zr[me_r] = zs[me_r]
-    fourth = scatter_sum(0, lambda stage: None)
+    third = scatter_sum(0, lambda stage: None)
     wait_rows(zr, 0)
     starts = {}
     blocks = n_row // 2
     p_change = None
     for c in range(2):
-        adj = finish_sum(0, c, fourth)
+        adj = finish_sum(0, c, third)
         rows = pl.ds(c * blocks, blocks)
         old = zr[rows, 0:st_local, :].reshape(tile, tile)
         cost = zr[rows, st_local : 2 * st_local, :].reshape(tile, tile)
@@ -299,14 +283,13 @@
         dual_out[r] = new
         moved = jnp.sum((new - old) ** 2, axis=0, keepdims=True)
         d_change = moved if d_change is None else d_change + moved
-    line = lax.broadcasted_iota(jnp.int32, (8, tile), 0)
-    ar_s[0] = jnp.where(
-        line == 0,
-        jnp.broadcast_to(p_change, (8, tile)),
-        jnp.where(line == 1, jnp.broadcast_to(d_change, (8, tile)), 0.0),
-    )
-
-    def send_change(i, carry):
+    lane = lax.broadcasted_iota(jnp.int32, (1, tile), 1)
+    p_change = p_change + pltpu.roll(p_change, tile // 2, 1)
+    d_change = d_change + pltpu.roll(d_change, tile // 2, 1)
+    ar_s[0] = jnp.where(lane < tile // 2, p_change, d_change)
+
+    def send_change(n, carry):
+        i = far_first(n)
         row_copy(ar_s.at[0], ar1.at[me_r], 1, i).start()
         return carry
 
@@ -315,36 +298,40 @@
 
     adjoint(1)
     counter[0] = MSGS
-    sides = {}
+
+    def cons_copy(i):
+        return pltpu.make_async_remote_copy(
+            src_ref=ar_s.at[1],
+            dst_ref=ar2.at[me_c],
+            send_sem=z_send.at[3],
+            recv_sem=z_recv.at[3],
+            device_id=(lax.rem(me_c + i, n_cons), me_r),
+            device_id_type=MESH,
+        )
+
+    def send_cons(i, carry):
+        cons_copy(i).start()
+        return carry
 
     def mids(stage):
         if stage == 0:
             wait_rows(ar1, 1)
-            total = ar1[0]
-            for i in range(1, n_row):
-                total = total + ar1[i]
+            total = jnp.sum(ar1[...], axis=0)
             ar_s[1] = total
-            ar2[x] = total
-            sides[0] = [send(ar_s.at[1], ar2.at[x], at_xy(y, x + i)) for i in range(1, SIDE)]
-        else:
-            for copy in sides[0]:
-                copy.wait_recv()
-            total = (ar2[0] + ar2[1]) + (ar2[2] + ar2[3])
-            ar_s[2] = total
-            ar3[y] = total
-            sides[1] = [send(ar_s.at[2], ar3.at[y], at_xy(y + i, x)) for i in range(1, SIDE)]
-
-    fourth = scatter_sum(1, mids)
-    for copy in sides[1]:
-        copy.wait_recv()
-    total = (ar3[0] + ar3[1]) + (ar3[2] + ar3[3])
-    p_total = jnp.sum(total[0:1], axis=1, keepdims=True)
-    d_total = jnp.sum(total[1:2], axis=1, keepdims=True)
+            ar2[me_c] = total
+            lax.fori_loop(1, n_cons, send_cons, 0)
+
+    third = scatter_sum(1, mids)
+    others = ar2.at[pl.ds(0, n_cons - 1)]
+    pltpu.make_async_copy(others, others, z_recv.at[3]).wait()
+    total = jnp.sum(ar2[...], axis=0)
+    p_total = jnp.sum(jnp.where(lane < tile // 2, total, 0.0), axis=1, keepdims=True)
+    d_total = jnp.sum(jnp.where(lane < tile // 2, 0.0, total), axis=1, keepdims=True)
     ratio = jnp.sqrt(jnp.sqrt((d_total + 1e-06) / (p_total + 1e-06)))
     p_step = step_scale / ratio
     d_step = step_scale * ratio
     for c in range(2):
-        adj = finish_sum(1, c, fourth)
+        adj = finish_sum(1, c, third)
         rows = pl.ds(c * blocks, blocks)
         old = newp[0, c]
         cost = zr[rows, st_local : 2 * st_local, :].reshape(tile, tile)
@@ -357,7 +344,8 @@
     def result_block(j):
         return newp.at[1, j // blocks, pl.ds((j % blocks) * st_local, st_local)]
 
-    def send_out(i, carry):
+    def send_out(n, carry):
+        i = far_first(n)
         row_copy(
             result_block(lax.rem(me_r + i, n_row)),
             outb.at[pl.ds(pl.multiple_of(me_r * st_local, st_local), st_local)],
@@ -383,6 +371,7 @@
         copy.wait_send()
     wait_rows_sent(zs, 0)
     wait_rows_sent(ar1, 1)
+    pltpu.make_async_copy(others, others, z_send.at[3]).wait()
     pltpu.make_async_copy(everything, everything, z_send.at[2]).wait()
 
 
@@ -419,14 +408,13 @@
     flat = (st_local * sku_local, scenes)
     smem = pl.BlockSpec(memory_space=pltpu.SMEM)
     vmem = pl.BlockSpec(memory_space=pltpu.VMEM)
-    total = 2 * MSGS + 2 * (SIDE - 1)
     primal, dual = pl.pallas_call(
-        functools.partial(kernel, n_row, slots),
+        functools.partial(kernel, n_row, n_cons, slots),
         out_shape=(
             jax.ShapeDtypeStruct(flat, F32),
             jax.ShapeDtypeStruct(start_dual.shape, F32),
         ),
-        in_specs=[smem, smem] + [vmem] * 6,
+        in_specs=[smem, smem] + [pl.BlockSpec(memory_space=pltpu.MemorySpace.HBM)] * 6,
         out_specs=(vmem, vmem),
         scratch_shapes=[
             pltpu.VMEM((n_row, 3 * st_local, scenes), F32),
@@ -438,22 +426,25 @@
             pltpu.VMEM((2, 2, 4, tile, scenes), F32),
             pltpu.VMEM((2, 2, 4, tile, scenes), F32),
             pltpu.VMEM((2, 2, 4, tile, scenes), F32),
-            pltpu.VMEM((2, 2, tile // 2, scenes), F32),
-            pltpu.VMEM((2, 2, tile // 2, scenes), F32),
-            pltpu.VMEM((2, 2, tile, scenes), F32),
-            pltpu.VMEM((2, 2, tile, scenes), F32),
+            pltpu.VMEM((2, 2, 3, tile, scenes), F32),
             pltpu.VMEM((2, n_cons, 2, tile, scenes), BF16),
             pltpu.VMEM((2, 2, tile, scenes), F32),
             pltpu.VMEM((stores, scenes), F32),
             pltpu.VMEM((2, 2, tile, scenes), BF16),
-            pltpu.VMEM((3, 8, scenes), F32),
-            pltpu.VMEM((n_row, 8, scenes), F32),
-            pltpu.VMEM((SIDE, 8, scenes), F32),
-            pltpu.VMEM((SIDE, 8, scenes), F32),
-            pltpu.SemaphoreType.DMA((total,)),
-            pltpu.SemaphoreType.DMA((total,)),
-            pltpu.SemaphoreType.DMA((3,)),
-            pltpu.SemaphoreType.DMA((3,)),
+            pltpu.VMEM((2, 1, scenes), F32),
+            pltpu.VMEM((n_row, 1, scenes), F32),
+            pltpu.VMEM((n_cons, 1, scenes), F32),
+            pltpu.SemaphoreType.DMA((2 * MSGS,)),
+            pltpu.SemaphoreType.DMA((2 * MSGS,)),
+            pltpu.SemaphoreType.DMA((4,)),
+            pltpu.SemaphoreType.DMA((4,)),
+            pltpu.VMEM(flat, F32),
+            pltpu.VMEM(flat, F32),
+            pltpu.VMEM(flat, F32),
+            pltpu.VMEM(start_dual.shape, F32),
+            pltpu.VMEM(demand.shape, F32),
+            pltpu.VMEM(tile_values.shape, BF16),
+            pltpu.SemaphoreType.DMA((6,)),
         ],
         compiler_params=pltpu.CompilerParams(
             collective_id=0, has_side_effects=True, vmem_limit_bytes=48 * 1024 * 1024

time: 97.7 us -> 88.2 us (0.903)
  Pallas kernels: 86.7 us -> 77.2 us
    pallas_call x1, Pallas kernels: 86.7 us -> 77.2 us  [body(): pl.pallas_call(functools.partial(kernel, n_row, n_cons, slots), out_shape...]
where the time goes in v2:
time: 88.2 us; the launch traced here: 87.2 us
  Pallas kernels  77.2 us (88%)
  local copies, waits for them, and re-layouts  8.25 us (9%)
  between operations  1.32 us (1%)
    pallas_call x1, Pallas kernels, body(): pl.pallas_call(functools.partial(kernel, n_row, n_cons, slots), out_shape...  77.2 us
    unnamed x18, local copies, waits for them, and re-layouts  8.16 us

profile of v2, /device:TPU:6, one launch (start us, length us, event | category | flops | bytes accessed | tf_op | source)
XLA Modules:
  0.0 87.2 jit_solution(8469414362193746176)
XLA Ops:
  1.3 0.0 copy-start.7
  1.3 0.6 copy-done.7
  1.9 0.1 select_reduce_fusion
  2.0 0.0 copy-start.6
  2.1 0.6 copy-done.6
  2.7 0.1 reshape.35.hot
  2.8 0.2 select_reduce_fusion.1
  3.0 0.1 pad_add_fusion.meta
  3.1 0.0 copy-start
  3.1 1.0 %copy-done = bf16[16,128,128]{2,1,0:T(8,128)(2,1)S(1)} copy-done((bf16[16,128,128]{2,1,0:T(8,128)(2,1)S(1)}, bf16[16,128,128]{2,1,0:T(8,128)(2,1)}, u32[]{:S(2)}) %copy-start) | copy-done | bytes 524312
  4.1 0.0 copy-start.1
  4.1 0.9 %copy-done.1 = f32[8,32,128]{2,1,0:T(8,128)S(1)} copy-done((f32[8,32,128]{2,1,0:T(8,128)S(1)}, f32[8,32,128]{2,1,0:T(8,128)}, u32[]{:S(2)}) %copy-start.1) | copy-done | bytes 131096
  5.0 0.0 copy-start.2
  5.0 0.9 %copy-done.2 = f32[8,32,128]{2,1,0:T(8,128)S(1)} copy-done((f32[8,32,128]{2,1,0:T(8,128)S(1)}, f32[8,32,128]{2,1,0:T(8,128)}, u32[]{:S(2)}) %copy-start.2) | copy-done | bytes 131096
  5.9 0.0 copy-start.3
  5.9 0.9 %copy-done.3 = f32[8,32,128]{2,1,0:T(8,128)S(1)} copy-done((f32[8,32,128]{2,1,0:T(8,128)S(1)}, f32[8,32,128]{2,1,0:T(8,128)}, u32[]{:S(2)}) %copy-start.3) | copy-done | bytes 131096
  6.8 0.0 copy-start.4
  6.8 0.9 %copy-done.4 = f32[2,128,128]{2,1,0:T(8,128)S(1)} copy-done((f32[2,128,128]{2,1,0:T(8,128)S(1)}, f32[2,128,128]{2,1,0:T(8,128)}, u32[]{:S(2)}) %copy-start.4) | copy-done | bytes 131096
  7.7 0.0 copy-start.5
  7.7 0.9 %copy-done.5 = f32[2,128,128]{2,1,0:T(8,128)S(1)} copy-done((f32[2,128,128]{2,1,0:T(8,128)S(1)}, f32[2,128,128]{2,1,0:T(8,128)}, u32[]{:S(2)}) %copy-start.5) | copy-done | bytes 131096
  8.6 77.2 %shard_map.104 = (f32[256,128]{1,0:T(8,128)S(1)}, f32[2,128,128]{2,1,0:T(8,128)S(1)}) custom-call(s32[80]{0:T(128)S(1)} %pad_add_fusion.meta, f32[32]{0:T(128)S(1)} %reshape.35.hot, f32[256,128]{1,0:T(8,128)S(1)} %bitcast.7, f32[256,128]{1,0:T(8,128)S(1)} %bitcast.8, f32[256,128]{1,0:T(8,128)S(1)} %bitcast.9, f32[2,128,128]{2,1,0:T(8,128)S(1)} %copy-done.4, ...), custom_call_target="tpu_custom_call" | custom-call | tf_op jit(solution)/shard_map/pallas_call | solution.py:411
  85.9 0.7 copy.14
  86.5 0.7 copy.15
  (4 shorter events, 0.0 us)
Async XLA Ops:
  1.3 0.7 copy-start.7
  2.0 0.7 copy-start.6
  3.1 1.0 %copy-start = (bf16[16,128,128]{2,1,0:T(8,128)(2,1)S(1)}, bf16[16,128,128]{2,1,0:T(8,128)(2,1)}, u32[]{:S(2)}) copy-start(bf16[16,128,128]{2,1,0:T(8,128)(2,1)} %tiles_hbm.1) | copy-start | bytes 1572868
  4.1 0.9 %copy-start.1 = (f32[8,32,128]{2,1,0:T(8,128)S(1)}, f32[8,32,128]{2,1,0:T(8,128)}, u32[]{:S(2)}) copy-start(f32[8,32,128]{2,1,0:T(8,128)} %param.9) | copy-start | bytes 393220
  5.0 0.9 %copy-start.2 = (f32[8,32,128]{2,1,0:T(8,128)S(1)}, f32[8,32,128]{2,1,0:T(8,128)}, u32[]{:S(2)}) copy-start(f32[8,32,128]{2,1,0:T(8,128)} %param.11) | copy-start | bytes 393220
  5.9 0.9 %copy-start.3 = (f32[8,32,128]{2,1,0:T(8,128)S(1)}, f32[8,32,128]{2,1,0:T(8,128)}, u32[]{:S(2)}) copy-start(f32[8,32,128]{2,1,0:T(8,128)} %param.12) | copy-start | bytes 393220
  6.8 0.9 %copy-start.4 = (f32[2,128,128]{2,1,0:T(8,128)S(1)}, f32[2,128,128]{2,1,0:T(8,128)}, u32[]{:S(2)}) copy-start(f32[2,128,128]{2,1,0:T(8,128)} %dual_hbm.1) | copy-start | bytes 393220
  7.7 0.9 %copy-start.5 = (f32[2,128,128]{2,1,0:T(8,128)S(1)}, f32[2,128,128]{2,1,0:T(8,128)}, u32[]{:S(2)}) copy-start(f32[2,128,128]{2,1,0:T(8,128)} %demand_hbm.1) | copy-start | bytes 393220

commit v3 on v2

--- a/solution.py
+++ b/solution.py
@@ -13,15 +13,16 @@
 MESH = pl.DeviceIdType.MESH
 F32 = jnp.float32
 BF16 = jnp.bfloat16
-MSGS = 68
+MSGS = 84
 
 
 def kernel(
     n_row,
     n_cons,
     slots,
-    meta,
-    hot,
+    rows_ref,
+    cols_ref,
+    count_ref,
     primal_hbm,
     cost_hbm,
     bound_hbm,
@@ -99,20 +100,14 @@
 
     barrier = pltpu.get_barrier_semaphore()
 
-    def greet(i, carry):
-        pl.semaphore_signal(
-            barrier, inc=1, device_id=(me_c, lax.rem(me_r + far_first(i), n_row)), device_id_type=MESH
-        )
+    def greet(n, carry):
+        peer = lax.rem(me_r + far_first(n), n_row)
+        pl.semaphore_signal(barrier, inc=1, device_id=(me_c, peer), device_id_type=MESH)
         return carry
 
-    def greet_cons(i, carry):
-        pl.semaphore_signal(
-            barrier, inc=1, device_id=(lax.rem(me_c + i, n_cons), me_r), device_id_type=MESH
-        )
-        return carry
-
     lax.fori_loop(1, n_row, greet, 0)
-    lax.fori_loop(1, n_cons, greet_cons, 0)
+    for peer in (x_next, x_prev, y_next, y_prev):
+        pl.semaphore_signal(barrier, inc=1, device_id=(peer, me_r), device_id_type=MESH)
 
     pending = []
     counter = [0]
@@ -132,6 +127,27 @@
         pending.append(copy)
         return copy
 
+    count = count_ref[0]
+    rows = [rows_ref[t] for t in range(slots)]
+    cols = [cols_ref[t] for t in range(slots)]
+    live = [jnp.where(t < count, cols[t], -1) for t in range(slots)]
+    before = []
+    for t in range(slots):
+        found = jnp.int32(slots)
+        for u in range(t):
+            found = jnp.where(cols[u] == cols[t], u, found)
+        before.append(found)
+    last_tile = []
+    for b in range(2 * n_cons):
+        found = jnp.int32(slots)
+        for t in range(slots):
+            found = jnp.where(live[t] == b, t, found)
+        last_tile.append(found)
+    hot = [
+        [jnp.where((rows[t] == r) & (t < count), 1.0, 0.0).astype(F32) for t in range(slots)]
+        for r in range(2)
+    ]
+
     for load in loads[2:5]:
         load.wait()
     for j in range(n_row):
@@ -143,53 +159,68 @@
             src = dual_in if it == 0 else dual_out
             dlow[it, r] = src[r].astype(BF16)
         for t in range(slots):
-            row = meta[slots + t]
             prod = lax.dot_general(
-                tiles[t], dlow[it, row], (((0,), (0,)), ((), ())), preferred_element_type=F32
+                tiles[t], dlow[it, rows[t]], (((0,), (0,)), ((), ())), preferred_element_type=F32
             )
-            chain[t] = prod + chain[meta[2 * slots + t]]
-        for b in range(2 * SIDE * SIDE):
-            part[it, b // 2, b % 2] = chain[meta[3 * slots + b]]
+            chain[t] = prod + chain[before[t]]
+        for b in range(2 * n_cons):
+            part[it, b // 2, b % 2] = chain[last_tile[b]]
 
     OFF = (2, 1, 3, 0)
     peers_a = [[at_xy(y, x + o), at_xy(y + o, x)] for o in range(SIDE)]
     peers_b = [[at_xy(y + o, x), at_xy(y, x + o)] for o in range(SIDE)]
 
-    def scatter_sum(it, mids):
-        first = {}
+    def scatter_sum(it, between):
+        lo, hi = pl.ds(0, half), pl.ds(half, half)
+        first, early, second = {}, {}, {}
+        third = {0: [], 1: []}
+
+        def chunk(k, c, step):
+            return blk(c, pos_b[c] + OFF[k], pos_a[c] + step)
+
+        def ahead(k):
+            for c in range(2):
+                up = part.at[it, chunk(k, c, 1), c]
+                down = part.at[it, chunk(k, c, 3), c]
+                early[k, c] = (
+                    send(up.at[hi], r2.at[it, c, k].at[hi], next_a[c]),
+                    send(down.at[lo], l2.at[it, c, k].at[lo], prev_a[c]),
+                )
+
         for k in range(4):
             for c in range(2):
-                opp = part.at[it, blk(c, pos_b[c] + OFF[k], pos_a[c] + 2), c]
-                a = send(opp.at[pl.ds(0, half)], r1.at[it, c, k], next_a[c])
-                b = send(opp.at[pl.ds(half, half)], l1.at[it, c, k], prev_a[c])
-                first[k, c] = (a, b)
-        second = {}
+                opp = part.at[it, chunk(k, c, 2), c]
+                first[k, c] = (
+                    send(opp.at[lo], r1.at[it, c, k], next_a[c]),
+                    send(opp.at[hi], l1.at[it, c, k], prev_a[c]),
+                )
+        ahead(0)
+        ahead(1)
+        between(0)
         for k in range(4):
             for c in range(2):
-                a, b = first[k, c]
-                nb = blk(c, pos_b[c] + OFF[k], pos_a[c] + 1)
-                a.wait_recv()
-                part[it, nb, c, 0:half, :] = part[it, nb, c, 0:half, :] + r1[it, c, k]
-                a2 = send(part.at[it, nb, c], r2.at[it, c, k], next_a[c])
-                pb = blk(c, pos_b[c] + OFF[k], pos_a[c] + 3)
-                b.wait_recv()
-                part[it, pb, c, half:tile, :] = part[it, pb, c, half:tile, :] + l1[it, c, k]
-                b2 = send(part.at[it, pb, c], l2.at[it, c, k], prev_a[c])
-                second[k, c] = (a2, b2)
-        mids(0)
-        third = {0: [], 1: []}
+                up, down = chunk(k, c, 1), chunk(k, c, 3)
+                first[k, c][0].wait_recv()
+                part[it, up, c, 0:half, :] = part[it, up, c, 0:half, :] + r1[it, c, k]
+                a = send(part.at[it, up, c].at[lo], r2.at[it, c, k].at[lo], next_a[c])
+                first[k, c][1].wait_recv()
+                part[it, down, c, half:tile, :] = part[it, down, c, half:tile, :] + l1[it, c, k]
+                b = send(part.at[it, down, c].at[hi], l2.at[it, c, k].at[hi], prev_a[c])
+                second[k, c] = (a, b)
+            if k < 2:
+                ahead(k + 2)
+            between(1 + k)
         for k in range(4):
             for c in range(2):
-                a, b = second[k, c]
-                a.wait_recv()
-                b.wait_recv()
-                own = blk(c, pos_b[c] + OFF[k], pos_a[c])
+                for copy in early[k, c] + second[k, c]:
+                    copy.wait_recv()
+                own = chunk(k, c, 0)
                 mid[it, c, k] = part[it, own, c] + r2[it, c, k] + l2[it, c, k]
                 if k < 3:
                     third[c].append(
                         send(mid.at[it, c, k], near.at[it, c, k], peers_b[OFF[k]][c])
                     )
-        mids(1)
+            between(5 + k)
         return third
 
     def finish_sum(it, c, third):
@@ -217,9 +248,9 @@
         acc = None
         for t in range(slots):
             prod = jnp.dot(
-                tiles[t], panel_at(it, meta[t]), preferred_element_type=F32
+                tiles[t], panel_at(it, cols[t]), preferred_element_type=F32
             )
-            prod = prod * hot[r * slots + t]
+            prod = prod * hot[r][t]
             acc = prod if acc is None else acc + prod
         return acc
 
@@ -231,7 +262,7 @@
     loads[1].wait()
     adjoint(0)
     loads[5].wait()
-    pl.semaphore_wait(barrier, (n_row - 1) + (n_cons - 1))
+    pl.semaphore_wait(barrier, n_row - 1 + 4)
 
     def row_copy(src, dst, group, i):
         return pltpu.make_async_remote_copy(
@@ -265,10 +296,10 @@
     p_change = None
     for c in range(2):
         adj = finish_sum(0, c, third)
-        rows = pl.ds(c * blocks, blocks)
-        old = zr[rows, 0:st_local, :].reshape(tile, tile)
-        cost = zr[rows, st_local : 2 * st_local, :].reshape(tile, tile)
-        bound = zr[rows, 2 * st_local : 3 * st_local, :].reshape(tile, tile)
+        span = pl.ds(c * blocks, blocks)
+        old = zr[span, 0:st_local, :].reshape(tile, tile)
+        cost = zr[span, st_local : 2 * st_local, :].reshape(tile, tile)
+        bound = zr[span, 2 * st_local : 3 * st_local, :].reshape(tile, tile)
         new = jnp.minimum(jnp.maximum(old - step_scale * (cost - adj), 0.0), bound)
         newp[0, c] = new
         panel[0, me_c, c] = (2.0 * new - old).astype(BF16)
@@ -313,15 +344,15 @@
         cons_copy(i).start()
         return carry
 
-    def mids(stage):
-        if stage == 0:
+    def between_second(stage):
+        if stage == 6:
             wait_rows(ar1, 1)
             total = jnp.sum(ar1[...], axis=0)
             ar_s[1] = total
             ar2[me_c] = total
             lax.fori_loop(1, n_cons, send_cons, 0)
 
-    third = scatter_sum(1, mids)
+    third = scatter_sum(1, between_second)
     others = ar2.at[pl.ds(0, n_cons - 1)]
     pltpu.make_async_copy(others, others, z_recv.at[3]).wait()
     total = jnp.sum(ar2[...], axis=0)
@@ -332,10 +363,10 @@
     d_step = step_scale * ratio
     for c in range(2):
         adj = finish_sum(1, c, third)
-        rows = pl.ds(c * blocks, blocks)
+        span = pl.ds(c * blocks, blocks)
         old = newp[0, c]
-        cost = zr[rows, st_local : 2 * st_local, :].reshape(tile, tile)
-        bound = zr[rows, 2 * st_local : 3 * st_local, :].reshape(tile, tile)
+        cost = zr[span, st_local : 2 * st_local, :].reshape(tile, tile)
+        bound = zr[span, 2 * st_local : 3 * st_local, :].reshape(tile, tile)
         new = jnp.minimum(jnp.maximum(old - p_step * (cost - adj), 0.0), bound)
         newp[1, c] = new
         panel[1, me_c, c] = (2.0 * new - old).astype(BF16)
@@ -392,19 +423,6 @@
     stores = st_local * n_row
     tile = tile_values.shape[1]
     slots = tile_values.shape[0]
-    panel_blocks = n_cons * stores // tile
-    order = jnp.arange(slots)
-    live = order < tile_count[0]
-    row_hot = (tile_rows[None, :] == jnp.arange(2)[:, None]) & live[None, :]
-    same = (tile_cols[None, :] == tile_cols[:, None]) & (order[None, :] < order[:, None])
-    before = jnp.max(jnp.where(same, order[None, :], -1), axis=1)
-    before = jnp.where(before < 0, slots, before)
-    holds = (tile_cols[None, :] == jnp.arange(panel_blocks)[:, None]) & live[None, :]
-    last = jnp.max(jnp.where(holds, order[None, :], -1), axis=1)
-    last = jnp.where(last < 0, slots, last)
-    meta = jnp.concatenate([tile_cols, tile_rows, before, last]).astype(jnp.int32)
-    hot = row_hot.astype(F32).reshape(-1)
-
     flat = (st_local * sku_local, scenes)
     smem = pl.BlockSpec(memory_space=pltpu.SMEM)
     vmem = pl.BlockSpec(memory_space=pltpu.VMEM)
@@ -414,7 +432,7 @@
             jax.ShapeDtypeStruct(flat, F32),
             jax.ShapeDtypeStruct(start_dual.shape, F32),
         ),
-        in_specs=[smem, smem] + [pl.BlockSpec(memory_space=pltpu.MemorySpace.HBM)] * 6,
+        in_specs=[smem, smem, smem] + [pl.BlockSpec(memory_space=pltpu.MemorySpace.HBM)] * 6,
         out_specs=(vmem, vmem),
         scratch_shapes=[
             pltpu.VMEM((n_row, 3 * st_local, scenes), F32),
@@ -447,11 +465,12 @@
             pltpu.SemaphoreType.DMA((6,)),
         ],
         compiler_params=pltpu.CompilerParams(
-            collective_id=0, has_side_effects=True, vmem_limit_bytes=48 * 1024 * 1024
+            collective_id=0, has_side_effects=True, vmem_limit_bytes=67_043_328
         ),
     )(
-        meta,
-        hot,
+        tile_rows,
+        tile_cols,
+        tile_count,
         start_primal.reshape(flat),
         unit_cost.reshape(flat),
         upper_bound.reshape(flat),

time: 88.2 us -> 82.5 us (0.935)
  local copies, waits for them, and re-layouts: 8.25 us -> 2.26 us
  Pallas kernels: 77.2 us -> 78.2 us
    unnamed x18 -> x4, local copies, waits for them, and re-layouts: 8.16 us -> 2.26 us
    pallas_call x1, Pallas kernels: 77.2 us -> 78.2 us  [body(): pl.pallas_call(functools.partial(kernel, n_row, n_cons, slots), out_shape...]
where the time goes in v3:
time: 82.5 us; the launch traced here: 81.8 us
  Pallas kernels  78.2 us (95%)
  local copies, waits for them, and re-layouts  2.26 us (3%)
  between operations  1.3 us (2%)
    pallas_call x1, Pallas kernels, body(): pl.pallas_call(functools.partial(kernel, n_row, n_cons, slots), out_shape...  78.2 us
    unnamed x4, local copies, waits for them, and re-layouts  2.26 us

profile of v3, /device:TPU:6, one launch (start us, length us, event | category | flops | bytes accessed | tf_op | source)
XLA Modules:
  0.0 81.8 jit_solution(10940441172131785549)
XLA Ops:
  1.3 78.2 %shard_map.104 = (f32[256,128]{1,0:T(8,128)}, f32[2,128,128]{2,1,0:T(8,128)}) custom-call(s32[16]{0:T(128)} %rows_ref.1, s32[16]{0:T(128)} %cols_ref.1, s32[1]{0:T(128)S(6)} %copy.13.count_ref, f32[256,128]{1,0:T(8,128)} %bitcast.4, f32[256,128]{1,0:T(8,128)} %bitcast.5, f32[256,128]{1,0:T(8,128)} %bitcast.6, f32[2,128,128]{2,1,0:T(8,128)} %dual_hbm.1, ...), custom_call_target="tpu_custom_call" | custom-call | tf_op jit(solution)/shard_map/pallas_call | solution.py:429
  79.5 0.0 copy-start
  79.5 1.6 %copy.14 = f32[8,32,128]{2,1,0:T(8,128)} copy(f32[8,32,128]{2,1,0:T(8,128)} %bitcast.7) | data formatting | bytes 262144
  81.1 0.0 copy-done
  81.1 0.7 copy.15
Async XLA Ops:
  79.5 1.6 %copy-start = (f32[2,128,128]{2,1,0:T(8,128)S(1)}, f32[2,128,128]{2,1,0:T(8,128)}, u32[]{:S(2)}) copy-start(f32[2,128,128]{2,1,0:T(8,128)} %get-tuple-element.9) | copy-start | bytes 393220

commit v4 on v3

--- a/solution.py
+++ b/solution.py
@@ -14,6 +14,24 @@
 F32 = jnp.float32
 BF16 = jnp.bfloat16
 MSGS = 84
+
+
+PRIMAL = (0.0, 1.0, 20)
+COST = (-6.0, 6.0, 22)
+BOUND = (0.5, 2.0, 20)
+SPLIT = 9
+
+
+def fixed(value, form):
+    low, high, bits = form
+    top = float((1 << bits) - 1)
+    code = (value - low) * (top / (high - low)) + 0.5
+    return jnp.clip(code, 0.0, top).astype(jnp.int32)
+
+
+def unfixed(code, form):
+    low, high, bits = form
+    return code.astype(F32) * ((high - low) / float((1 << bits) - 1)) + low
 
 
 def kernel(
@@ -151,8 +169,13 @@
     for load in loads[2:5]:
         load.wait()
     for j in range(n_row):
-        for k, ref in enumerate((primal_in, cost_in, bound_in)):
-            zs[j, k * st_local : (k + 1) * st_local, :] = ref[pl.ds(j, st_local, stride=n_row), :]
+        stores = pl.ds(j, st_local, stride=n_row)
+        start = fixed(primal_in[stores, :], PRIMAL)
+        cost = fixed(cost_in[stores, :], COST)
+        bound = fixed(bound_in[stores, :], BOUND)
+        zs[j, 0:st_local, :] = cost * (1 << SPLIT) + (bound >> (BOUND[2] - SPLIT))
+        rest = bound & ((1 << (BOUND[2] - SPLIT)) - 1)
+        zs[j, st_local : 2 * st_local, :] = rest * (1 << PRIMAL[2]) + start
 
     def adjoint(it):
         for r in range(2):
@@ -287,19 +310,30 @@
         everything = buf.at[pl.ds(0, n_row - 1)]
         pltpu.make_async_copy(everything, everything, z_send.at[group]).wait()
 
+    blocks = n_row // 2
+
+    def owned(c):
+        span = pl.ds(c * blocks, blocks)
+        high = zr[span, 0:st_local, :].reshape(tile, tile)
+        low = zr[span, st_local : 2 * st_local, :].reshape(tile, tile)
+        rest_bits = BOUND[2] - SPLIT
+        bound = (high & ((1 << SPLIT) - 1)) * (1 << rest_bits) + (low >> PRIMAL[2])
+        start = low & ((1 << PRIMAL[2]) - 1)
+        return (
+            unfixed(start, PRIMAL),
+            unfixed(high >> SPLIT, COST),
+            unfixed(bound, BOUND),
+        )
+
     lax.fori_loop(1, n_row, send_in, 0)
     zr[me_r] = zs[me_r]
     third = scatter_sum(0, lambda stage: None)
     wait_rows(zr, 0)
     starts = {}
-    blocks = n_row // 2
     p_change = None
     for c in range(2):
         adj = finish_sum(0, c, third)
-        span = pl.ds(c * blocks, blocks)
-        old = zr[span, 0:st_local, :].reshape(tile, tile)
-        cost = zr[span, st_local : 2 * st_local, :].reshape(tile, tile)
-        bound = zr[span, 2 * st_local : 3 * st_local, :].reshape(tile, tile)
+        old, cost, bound = owned(c)
         new = jnp.minimum(jnp.maximum(old - step_scale * (cost - adj), 0.0), bound)
         newp[0, c] = new
         panel[0, me_c, c] = (2.0 * new - old).astype(BF16)
@@ -363,10 +397,8 @@
     d_step = step_scale * ratio
     for c in range(2):
         adj = finish_sum(1, c, third)
-        span = pl.ds(c * blocks, blocks)
         old = newp[0, c]
-        cost = zr[span, st_local : 2 * st_local, :].reshape(tile, tile)
-        bound = zr[span, 2 * st_local : 3 * st_local, :].reshape(tile, tile)
+        _, cost, bound = owned(c)
         new = jnp.minimum(jnp.maximum(old - p_step * (cost - adj), 0.0), bound)
         newp[1, c] = new
         panel[1, me_c, c] = (2.0 * new - old).astype(BF16)
@@ -404,6 +436,10 @@
     wait_rows_sent(ar1, 1)
     pltpu.make_async_copy(others, others, z_send.at[3]).wait()
     pltpu.make_async_copy(everything, everything, z_send.at[2]).wait()
+
+
+def pin(array):
+    return pltpu.with_memory_space_constraint(array, pltpu.MemorySpace.HBM)
 
 
 def body(
@@ -435,8 +471,8 @@
         in_specs=[smem, smem, smem] + [pl.BlockSpec(memory_space=pltpu.MemorySpace.HBM)] * 6,
         out_specs=(vmem, vmem),
         scratch_shapes=[
-            pltpu.VMEM((n_row, 3 * st_local, scenes), F32),
-            pltpu.VMEM((n_row, 3 * st_local, scenes), F32),
+            pltpu.VMEM((n_row, 2 * st_local, scenes), jnp.int32),
+            pltpu.VMEM((n_row, 2 * st_local, scenes), jnp.int32),
             pltpu.VMEM((slots + 1, tile, scenes), F32),
             pltpu.VMEM((2, n_cons, 2, tile, scenes), F32),
             pltpu.VMEM((2, 2, 4, tile // 2, scenes), F32),
@@ -465,18 +501,18 @@
             pltpu.SemaphoreType.DMA((6,)),
         ],
         compiler_params=pltpu.CompilerParams(
-            collective_id=0, has_side_effects=True, vmem_limit_bytes=67_043_328
+            collective_id=0, has_side_effects=True, vmem_limit_bytes=50_000_000
         ),
     )(
         tile_rows,
         tile_cols,
         tile_count,
-        start_primal.reshape(flat),
-        unit_cost.reshape(flat),
-        upper_bound.reshape(flat),
-        start_dual,
-        demand,
-        tile_values,
+        pin(start_primal.reshape(flat)),
+        pin(unit_cost.reshape(flat)),
+        pin(upper_bound.reshape(flat)),
+        pin(start_dual),
+        pin(demand),
+        pin(tile_values),
     )
     return (primal.reshape(start_primal.shape), dual)
 

time: 82.5 us -> 75.7 us (0.918)
  Pallas kernels: 78.2 us -> 71.4 us
    pallas_call x1, Pallas kernels: 78.2 us -> 71.4 us  [body(): pl.pallas_call(functools.partial(kernel, n_row, n_cons, slots), out_shape...]
    unnamed x4 -> x6, local copies, waits for them, and re-layouts: 2.26 us -> 1.97 us
where the time goes in v4:
time: 75.7 us; the launch traced here: 74.7 us
  Pallas kernels  71.4 us (94%)
  local copies, waits for them, and re-layouts  1.97 us (3%)
  between operations  1.3 us (2%)
    pallas_call x1, Pallas kernels, body(): pl.pallas_call(functools.partial(kernel, n_row, n_cons, slots), out_shape...  71.4 us
    unnamed x6, local copies, waits for them, and re-layouts  1.97 us

profile of v4, /device:TPU:6, one launch (start us, length us, event | category | flops | bytes accessed | tf_op | source)
XLA Modules:
  0.0 74.7 jit_solution(16932968455522995397)
XLA Ops:
  1.3 0.0 copy-start
  1.3 0.0 copy-start.1
  1.3 0.6 copy-done
  1.9 0.0 copy-done.1
  2.0 71.4 %shard_map.104 = (f32[256,128]{1,0:T(8,128)S(1)}, f32[2,128,128]{2,1,0:T(8,128)S(1)}) custom-call(s32[16]{0:T(128)S(1)} %copy-done, s32[16]{0:T(128)S(1)} %copy-done.1, s32[1]{0:T(128)S(6)} %copy.13.count_ref, f32[256,128]{1,0:T(8,128)} %bitcast.5, f32[256,128]{1,0:T(8,128)} %bitcast.6, f32[256,128]{1,0:T(8,128)} %bitcast.7, f32[2,128,128]{2,1,0:T(8,128)} %dual_hbm.1, ...), custom_call_target="tpu_custom_call" | custom-call | tf_op jit(solution)/shard_map/pallas_call | solution.py:465
  73.4 0.7 copy.14
  74.1 0.7 copy.15
Async XLA Ops:
  1.3 0.7 copy-start
  1.3 0.7 copy-start.1

commit v5 on v4

--- a/solution.py
+++ b/solution.py
@@ -210,17 +210,15 @@
                     send(down.at[lo], l2.at[it, c, k].at[lo], prev_a[c]),
                 )
 
-        for k in range(4):
+        def across(k):
             for c in range(2):
                 opp = part.at[it, chunk(k, c, 2), c]
                 first[k, c] = (
                     send(opp.at[lo], r1.at[it, c, k], next_a[c]),
                     send(opp.at[hi], l1.at[it, c, k], prev_a[c]),
                 )
-        ahead(0)
-        ahead(1)
-        between(0)
-        for k in range(4):
+
+        def relay(k):
             for c in range(2):
                 up, down = chunk(k, c, 1), chunk(k, c, 3)
                 first[k, c][0].wait_recv()
@@ -230,10 +228,8 @@
                 part[it, down, c, half:tile, :] = part[it, down, c, half:tile, :] + l1[it, c, k]
                 b = send(part.at[it, down, c].at[hi], l2.at[it, c, k].at[hi], prev_a[c])
                 second[k, c] = (a, b)
-            if k < 2:
-                ahead(k + 2)
-            between(1 + k)
-        for k in range(4):
+
+        def combine(k):
             for c in range(2):
                 for copy in early[k, c] + second[k, c]:
                     copy.wait_recv()
@@ -243,7 +239,24 @@
                     third[c].append(
                         send(mid.at[it, c, k], near.at[it, c, k], peers_b[OFF[k]][c])
                     )
-            between(5 + k)
+
+        across(0)
+        across(1)
+        across(2)
+        ahead(0)
+        ahead(1)
+        relay(0)
+        ahead(2)
+        relay(1)
+        relay(2)
+        across(3)
+        ahead(3)
+        combine(0)
+        combine(1)
+        between()
+        combine(2)
+        relay(3)
+        combine(3)
         return third
 
     def finish_sum(it, c, third):
@@ -327,7 +340,7 @@
 
     lax.fori_loop(1, n_row, send_in, 0)
     zr[me_r] = zs[me_r]
-    third = scatter_sum(0, lambda stage: None)
+    third = scatter_sum(0, lambda: None)
     wait_rows(zr, 0)
     starts = {}
     p_change = None
@@ -378,13 +391,12 @@
         cons_copy(i).start()
         return carry
 
-    def between_second(stage):
-        if stage == 6:
-            wait_rows(ar1, 1)
-            total = jnp.sum(ar1[...], axis=0)
-            ar_s[1] = total
-            ar2[me_c] = total
-            lax.fori_loop(1, n_cons, send_cons, 0)
+    def between_second():
+        wait_rows(ar1, 1)
+        total = jnp.sum(ar1[...], axis=0)
+        ar_s[1] = total
+        ar2[me_c] = total
+        lax.fori_loop(1, n_cons, send_cons, 0)
 
     third = scatter_sum(1, between_second)
     others = ar2.at[pl.ds(0, n_cons - 1)]
@@ -504,8 +516,8 @@
             collective_id=0, has_side_effects=True, vmem_limit_bytes=50_000_000
         ),
     )(
-        tile_rows,
-        tile_cols,
+        pin(tile_rows),
+        pin(tile_cols),
         tile_count,
         pin(start_primal.reshape(flat)),
         pin(unit_cost.reshape(flat)),

time: 75.7 us -> 75 us (level)
    unnamed x6 -> x2, local copies, waits for them, and re-layouts: 1.97 us -> 1.31 us
where the time goes in v5:
time: 75 us; the launch traced here: 74.4 us
  Pallas kernels  71.8 us (96%)
  local copies, waits for them, and re-layouts  1.31 us (2%)
  between operations  1.29 us (2%)
    pallas_call x1, Pallas kernels, body(): pl.pallas_call(functools.partial(kernel, n_row, n_cons, slots), out_shape...  71.8 us

profile of v5, /device:TPU:6, one launch (start us, length us, event | category | flops | bytes accessed | tf_op | source)
XLA Modules:
  0.0 74.4 jit_solution(4769829744960835132)
XLA Ops:
  1.3 71.8 %shard_map.104 = (f32[256,128]{1,0:T(8,128)S(1)}, f32[2,128,128]{2,1,0:T(8,128)S(1)}) custom-call(s32[16]{0:T(128)} %rows_ref.1, s32[16]{0:T(128)} %cols_ref.1, s32[1]{0:T(128)S(6)} %copy.13.count_ref, f32[256,128]{1,0:T(8,128)} %bitcast.5, f32[256,128]{1,0:T(8,128)} %bitcast.6, f32[256,128]{1,0:T(8,128)} %bitcast.7, f32[2,128,128]{2,1,0:T(8,128)} %dual_hbm.1, ...), custom_call_target="tpu_custom_call" | custom-call | tf_op jit(solution)/shard_map/pallas_call | solution.py:477
  73.1 0.7 copy.14
  73.8 0.7 copy.15

commit v6 on v5

--- a/solution.py
+++ b/solution.py
@@ -13,7 +13,7 @@
 MESH = pl.DeviceIdType.MESH
 F32 = jnp.float32
 BF16 = jnp.bfloat16
-MSGS = 84
+MSGS = 86
 
 
 PRIMAL = (0.0, 1.0, 20)
@@ -193,7 +193,7 @@
     peers_a = [[at_xy(y, x + o), at_xy(y + o, x)] for o in range(SIDE)]
     peers_b = [[at_xy(y + o, x), at_xy(y, x + o)] for o in range(SIDE)]
 
-    def scatter_sum(it, between):
+    def scatter_sum(it, begin, between):
         lo, hi = pl.ds(0, half), pl.ds(half, half)
         first, early, second = {}, {}, {}
         third = {0: [], 1: []}
@@ -245,6 +245,7 @@
         across(2)
         ahead(0)
         ahead(1)
+        begin()
         relay(0)
         ahead(2)
         relay(1)
@@ -267,7 +268,7 @@
     def gather_start(it, c):
         own = panel.at[it, me_c, c]
         deep = [send(own, own, peers_b[OFF[k]][c]) for k in range(3)]
-        wide = [send(own, own, peers_a[OFF[k]][c]) for k in range(3)]
+        wide = [send(own, own, peers_a[OFF[k]][c]) for k in (1, 2)]
         return deep, wide
 
     def gather_rest(it, starts):
@@ -277,18 +278,26 @@
                 starts[c][0][k].wait_recv()
                 piece = panel.at[it, blk(c, pos_b[c] + SIDE - OFF[k], pos_a[c]), c]
                 wide += [send(piece, piece, peers_a[OFF[j]][c]) for j in range(3)]
-        for copy in starts[0][1] + starts[1][1] + wide:
+            if k == 1:
+                for c in range(2):
+                    from_prev, from_next = starts[c][1]
+                    from_prev.wait_recv()
+                    piece = panel.at[it, blk(c, pos_b[c], pos_a[c] + 3), c].at[pl.ds(0, half)]
+                    wide.append(send(piece, piece, next_a[c]))
+                    from_next.wait_recv()
+                    piece = panel.at[it, blk(c, pos_b[c], pos_a[c] + 1), c].at[pl.ds(half, half)]
+                    wide.append(send(piece, piece, prev_a[c]))
+        for copy in wide:
             copy.wait_recv()
 
-    def forward(it, r):
-        acc = None
+    def forward(it):
+        sums = [None, None]
         for t in range(slots):
-            prod = jnp.dot(
-                tiles[t], panel_at(it, cols[t]), preferred_element_type=F32
-            )
-            prod = prod * hot[r][t]
-            acc = prod if acc is None else acc + prod
-        return acc
+            prod = jnp.dot(tiles[t], panel_at(it, cols[t]), preferred_element_type=F32)
+            for r in range(2):
+                term = prod * hot[r][t]
+                sums[r] = term if t == 0 else sums[r] + term
+        return sums
 
     def panel_at(it, col):
         return panel[it, col // 2, col % 2]
@@ -340,7 +349,7 @@
 
     lax.fori_loop(1, n_row, send_in, 0)
     zr[me_r] = zs[me_r]
-    third = scatter_sum(0, lambda: None)
+    third = scatter_sum(0, lambda: None, lambda: None)
     wait_rows(zr, 0)
     starts = {}
     p_change = None
@@ -355,9 +364,10 @@
         p_change = moved if p_change is None else p_change + moved
     gather_rest(0, starts)
     d_change = None
+    product = forward(0)
     for r in range(2):
         old = dual_in[r]
-        new = jnp.maximum(old + step_scale * (demand_in[r] - forward(0, r)), 0.0)
+        new = jnp.maximum(old + step_scale * (demand_in[r] - product[r]), 0.0)
         dual_out[r] = new
         moved = jnp.sum((new - old) ** 2, axis=0, keepdims=True)
         d_change = moved if d_change is None else d_change + moved
@@ -371,8 +381,9 @@
         row_copy(ar_s.at[0], ar1.at[me_r], 1, i).start()
         return carry
 
-    lax.fori_loop(1, n_row, send_change, 0)
-    ar1[me_r] = ar_s[0]
+    def begin_second():
+        lax.fori_loop(1, n_row, send_change, 0)
+        ar1[me_r] = ar_s[0]
 
     adjoint(1)
     counter[0] = MSGS
@@ -398,7 +409,7 @@
         ar2[me_c] = total
         lax.fori_loop(1, n_cons, send_cons, 0)
 
-    third = scatter_sum(1, between_second)
+    third = scatter_sum(1, begin_second, between_second)
     others = ar2.at[pl.ds(0, n_cons - 1)]
     pltpu.make_async_copy(others, others, z_recv.at[3]).wait()
     total = jnp.sum(ar2[...], axis=0)
@@ -434,9 +445,10 @@
         1, me_r // blocks, pl.ds(pl.multiple_of((me_r % blocks) * st_local, st_local), st_local), :
     ]
     gather_rest(1, starts)
+    product = forward(1)
     for r in range(2):
         dual_out[r] = jnp.maximum(
-            dual_out[r] + d_step * (demand_in[r] - forward(1, r)), 0.0
+            dual_out[r] + d_step * (demand_in[r] - product[r]), 0.0
         )
     everything = outb.at[pl.ds(0, (n_row - 1) * st_local)]
     pltpu.make_async_copy(everything, everything, z_recv.at[2]).wait()

time: 75 us -> 73.7 us (0.983)
  Pallas kernels: 71.8 us -> 70.4 us
    pallas_call x1, Pallas kernels: 71.8 us -> 70.4 us  [body(): pl.pallas_call(functools.partial(kernel, n_row, n_cons, slots), out_shape...]
where the time goes in v6:
time: 73.7 us; the launch traced here: 73 us
  Pallas kernels  70.4 us (96%)
  local copies, waits for them, and re-layouts  1.31 us (2%)
  between operations  1.29 us (2%)
    pallas_call x1, Pallas kernels, body(): pl.pallas_call(functools.partial(kernel, n_row, n_cons, slots), out_shape...  70.4 us

profile of v6, /device:TPU:6, one launch (start us, length us, event | category | flops | bytes accessed | tf_op | source)
XLA Modules:
  0.0 73.0 jit_solution(3698670068306507614)
XLA Ops:
  1.3 70.4 %shard_map.104 = (f32[256,128]{1,0:T(8,128)S(1)}, f32[2,128,128]{2,1,0:T(8,128)S(1)}) custom-call(s32[16]{0:T(128)} %rows_ref.1, s32[16]{0:T(128)} %cols_ref.1, s32[1]{0:T(128)S(6)} %copy.13.count_ref, f32[256,128]{1,0:T(8,128)} %bitcast.5, f32[256,128]{1,0:T(8,128)} %bitcast.6, f32[256,128]{1,0:T(8,128)} %bitcast.7, f32[2,128,128]{2,1,0:T(8,128)} %dual_hbm.1, ...), custom_call_target="tpu_custom_call" | custom-call | tf_op jit(solution)/shard_map/pallas_call | solution.py:489
  71.7 0.7 copy.14
  72.4 0.7 copy.15
